TPU v7x, 32 devices: a whole 2x2x4 slice. The times are simulated.
32 devices in a mesh: grp: 8 (over y, x, core), top: 4 (over z).
Axes of the slice: x: 2, y: 2, z: 4, core: 2. Of those that a mesh axis runs over, the one named last changes fastest.
Arguments:
- basis_grad: float32 [8, 4, 512, 384], P('grp', 'top'), may hold values from -6 to 6
- leaf_q: float32 [8, 4, 512, 384], P('grp', 'top'), may hold values from -0.25 to 0.25
- leaf_rinv: float32 [8, 4, 384, 384], P('grp', 'top'), may hold values from -5 to 4, as said below
- merge_q1: float32 [8, 4, 384, 384], P('grp', 'top'), may hold values from -0.3125 to 0.3125
- merge_q2: float32 [4, 384, 384], P('top', 'grp'), may hold values from -0.15625 to 0.15625
Outputs:
- data_grad: float32 [8, 4, 512, 384], P('grp', 'top')
Inputs may be any that keep to these rules, and one draw needn't show every extreme that they name: Each leaf_rinv[i,g] is upper triangular with a diagonal between 1 and 4.
All inputs are finite; a program needn't handle non-finite values.
Results may differ from a plain program's by a relative error of at most 0.00023.
Values sent between devices are 32-bit elements; how exact they have to be, the bound alone decides.
A program may use at most 64 MiB of HBM per device.

v0:
```python
import jax
import jax.numpy as jnp
from jax import lax
from jax.sharding import PartitionSpec as P


def product(former, latter, former_dim, latter_dim):
    return lax.dot_general(
        former,
        latter,
        (((former_dim,), (latter_dim,)), ((), ())),
        precision=lax.Precision.HIGH,
        preferred_element_type=jnp.float32,
    )


def symmetrize(matrix):
    return jnp.tril(matrix) + jnp.tril(matrix, -1).T


def per_device(basis_grad, leaf_q, leaf_rinv, merge_q1, merge_q2):
    cotangent = basis_grad[0, 0]
    leaf_basis = leaf_q[0, 0]
    inverse = leaf_rinv[0, 0]
    first_block = merge_q1[0, 0]
    second_factor = lax.all_gather(merge_q2[0], "grp", axis=0, tiled=True)
    projected = product(leaf_basis, cotangent, 0, 0)
    combined = product(first_block, second_factor, 1, 0)
    top_adjoint = -lax.psum(product(projected, combined, 0, 0), ("grp", "top"))
    top_sym = symmetrize(top_adjoint)
    spread = product(leaf_basis, combined, 1, 0)
    outer = product(inverse, combined, 1, 0)
    inner = cotangent + product(spread, top_sym, 1, 0)
    result = product(inner, outer, 1, 1)
    return result[None, None]


def solution(mesh):
    placed = (
        P("grp", "top", None, None),
        P("grp", "top", None, None),
        P("grp", "top", None, None),
        P("grp", "top", None, None),
        P("top", "grp", None),
    )
    return jax.shard_map(
        per_device,
        mesh=mesh,
        in_specs=placed,
        out_specs=P("grp", "top", None, None),
        check_vma=False,
    )
```

profile of v0, /device:TPU:0, one launch (start us, length us, event | category | flops | bytes accessed | tf_op | source)
XLA Modules:
  0.0 163.3 jit_solution(13517483141683757118)
XLA Ops:
  6.5 0.0 copy-start
  6.5 0.0 copy-start.2
  6.5 0.0 all-reduce.2.cloned.1.call-start
  6.5 11.9 %all-gather = f32[1,384,384]{2,1,0:T(8,128)S(1)} all-gather(f32[1,48,384]{2,1,0:T(8,128)} %param.9), channel_id=2, replica_groups=mesh['grp'=8,'top'=4] {'grp'}, dimensions={1}, use_global_device_ids=true | all-gather | bytes 663552 | tf_op jit(solution)/shard_map/all_gather | solution.py:26
  18.4 0.0 copy-done.2
  18.4 0.0 copy-start.1
  18.4 0.7 fusion.7
  19.2 0.0 copy-done
  19.2 0.4 copy-done.1
  19.6 0.8 fusion
  20.4 1.6 fusion.17
  22.0 0.0 copy-start.3
  22.0 0.0 all-reduce.2.cloned.1.call-update
  22.0 1.0 copy-done.3
  23.0 1.1 fusion.5
  24.2 1.2 fusion.2
  25.3 124.4 %all-reduce.2.cloned.1.call-done = f32[384,384]{1,0:T(8,128)} async-done(((f32[384,384]{1,0:T(8,128)}), f32[384,384]{1,0:T(8,128)}) %all-reduce.2.cloned.1.call-update) | async-done | bytes 589840 | tf_op jit(solution)/shard_map/psum | solution.py:29
  149.8 1.1 neg.3
  150.9 1.1 copy.6
  151.9 2.7 %convolution_add_fusion = f32[512,384]{1,0:T(8,128)S(1)} fusion(f32[384,512]{1,0:T(8,128)S(1)} %fusion.2, f32[1,1,512,384]{3,2,1,0:T(8,128)S(1)} %copy-done.1, f32[384,384]{0,1:T(8,128)} %copy.6, s32[384]{0:T(512)S(1)} %iota_add_fusion, f32[384,384]{1,0:T(8,128)} %all-reduce.2.cloned.1.call-done), kind=kOutput, calls=%fused_computation.1 | convolution fusion | flops 454066176 | bytes 3540480 | tf_op jit(solution)/shard_map/dot_general | solution.py:8
  154.7 1.8 %convolution_bitcast_fusion = f32[1,1,512,384]{3,2,1,0:T(8,128)} fusion(f32[512,384]{1,0:T(8,128)S(1)} %convolution_add_fusion, f32[384,384]{1,0:T(8,128)S(1)} %fusion.5), kind=kOutput, calls=%fused_computation | convolution fusion | flops 452984832 | bytes 2162688 | tf_op jit(solution)/shard_map/dot_general | solution.py:8
  (1 shorter events, 0.0 us)
Async XLA Ops:
  6.5 12.6 %copy-start = (f32[1,1,512,384]{3,2,1,0:T(8,128)S(1)}, f32[1,1,512,384]{3,2,1,0:T(8,128)}, u32[]{:S(2)}) copy-start(f32[1,1,512,384]{3,2,1,0:T(8,128)} %param.6) | copy-start | bytes 2359300
  6.5 11.9 %copy-start.2 = (f32[1,1,384,384]{3,2,1,0:T(8,128)S(1)}, f32[1,1,384,384]{3,2,1,0:T(8,128)}, u32[]{:S(2)}) copy-start(f32[1,1,384,384]{3,2,1,0:T(8,128)} %param.8) | copy-start | bytes 1769476
  6.5 143.2 %all-reduce.2.cloned.1.call-start = ((), (), s32[]{:S(2)}) async-start(), calls=%async_computation | async-start | bytes 1179648 | tf_op jit(solution)/shard_map/psum | solution.py:29
  18.4 1.1 copy-start.1
  22.0 1.1 copy-start.3
Sparse Core Ops, SparseCore 0:
  22.1 127.6 all-reduce.1
where the time goes:
time: 164 us; the launch traced here: 163 us
  waiting for transfers between devices  124 us (76%)
  between operations  13.4 us (8%)
  blocking collectives  11.9 us (7%)
  matrix products  9.86 us (6%)
  local copies, waits for them, and re-layouts  2.51 us (2%)
    psum x1, waiting for transfers between devices, per_device(): top_adjoint = -lax.psum(product(projected, combined, 0, 0), ('grp', 'top'))  124 us
    all_gather x1, blocking collectives, per_device(): second_factor = lax.all_gather(merge_q2[0], 'grp', axis=0, tiled=True)  11.9 us
    dot_general x7, matrix products, product(): lax.dot_general(former, latter, (((former_dim,), (latter_dim,)), ((), ())...  9.86 us
  transfers between devices with their start and end apart: 1, of which 1 were waited for; matrix products, arithmetic and copies ran while one was open for 1% of the time, Pallas kernels for 0%

commit v1 on v0

--- a/solution.py
+++ b/solution.py
@@ -2,6 +2,27 @@
 import jax.numpy as jnp
 from jax import lax
 from jax.sharding import PartitionSpec as P
+
+
+def collect(shard, axis, dim):
+    size, index, rows = (lax.axis_size(axis), lax.axis_index(axis), shard.shape[dim])
+    forward = [(i, (i + 1) % size) for i in range(size)]
+    left = [(i, (i - 1) % size) for i in range(size)]
+    out = jnp.zeros((*shard.shape[:dim], size * rows, *shard.shape[dim + 1 :]), shard.dtype)
+    out = lax.dynamic_update_slice_in_dim(out, shard, index * rows, axis=dim)
+    from_left = from_right = shard
+    half = size // 2
+    for step in range(1, half + 1):
+        from_left = lax.ppermute(from_left, axis, forward)
+        out = lax.dynamic_update_slice_in_dim(
+            out, from_left, (index - step) % size * rows, axis=dim
+        )
+        if step < size - half:
+            from_right = lax.ppermute(from_right, axis, left)
+            out = lax.dynamic_update_slice_in_dim(
+                out, from_right, (index + step) % size * rows, axis=dim
+            )
+    return out
 
 
 def product(former, latter, former_dim, latter_dim):
@@ -23,7 +44,7 @@
     leaf_basis = leaf_q[0, 0]
     inverse = leaf_rinv[0, 0]
     first_block = merge_q1[0, 0]
-    second_factor = lax.all_gather(merge_q2[0], "grp", axis=0, tiled=True)
+    second_factor = collect(merge_q2[0], "grp", 0)
     projected = product(leaf_basis, cotangent, 0, 0)
     combined = product(first_block, second_factor, 1, 0)
     top_adjoint = -lax.psum(product(projected, combined, 0, 0), ("grp", "top"))

time: 164 us -> 189 us (1.15)
  local copies, waits for them, and re-layouts: 2.51 us -> 16.8 us
  waiting for transfers between devices: 124 us -> 137 us
  blocking collectives: 11.9 us -> 0 us
  starting transfers between devices: 0.01 us -> 8.69 us
    dynamic_update_slice x0 -> x8, local copies, waits for them, and re-layouts: none -> 13.5 us  [the longest x4 6.02 us: collect(): lax.dynamic_update_slice_in_dim(out, from_left, (index - step) % size * r...]
    all_gather x1 -> x0, blocking collectives: 11.9 us -> none  [per_device(): second_factor = lax.all_gather(merge_q2[0], 'grp', axis=0, tiled=True)]
    ppermute x0 -> x7, starting transfers between devices: none -> 8.68 us  [the longest x3 8.12 us: collect(): from_right = lax.ppermute(from_right, axis, left)]
    psum x1, waiting for transfers between devices: 124 us -> 131 us  [per_device(): top_adjoint = -lax.psum(product(projected, combined, 0, 0), ('grp', 'top'))]
    ppermute x0 -> x7, waiting for transfers between devices: none -> 6.46 us  [the longest x4 5.54 us: collect(): from_left = lax.ppermute(from_left, axis, forward)]
  transfers between devices with their start and end apart: 1 -> 8, of which waited for: 1 -> 4; matrix products, arithmetic and copies ran while one was open for 1% -> 8% of each run, Pallas kernels for 0% -> 0%
where the time goes in v1:
time: 189 us; the launch traced here: 188 us
  waiting for transfers between devices  137 us (72%)
  local copies, waits for them, and re-layouts  16.8 us (9%)
  between operations  13.7 us (7%)
  matrix products  10.6 us (6%)
  starting transfers between devices  8.69 us (5%)
    psum x1, waiting for transfers between devices, per_device(): top_adjoint = -lax.psum(product(projected, combined, 0, 0), ('grp', 'top'))  131 us
    dot_general x7, matrix products, product(): lax.dot_general(former, latter, (((former_dim,), (latter_dim,)), ((), ())...  10.6 us
    ppermute x3, starting transfers between devices, collect(): from_right = lax.ppermute(from_right, axis, left)  8.12 us
    dynamic_update_slice x4, local copies, waits for them, and re-layouts, collect(): lax.dynamic_update_slice_in_dim(out, from_left, (index - step) % size * r...  6.02 us
    dynamic_update_slice x3, local copies, waits for them, and re-layouts, collect(): lax.dynamic_update_slice_in_dim(out, from_right, (index + step) % size *...  5.99 us
    ppermute x4, waiting for transfers between devices, collect(): from_left = lax.ppermute(from_left, axis, forward)  5.54 us
  transfers between devices with their start and end apart: 8, of which 4 were waited for; matrix products, arithmetic and copies ran while one was open for 8% of the time, Pallas kernels for 0%

profile of v1, /device:TPU:0, one launch (start us, length us, event | category | flops | bytes accessed | tf_op | source)
XLA Modules:
  0.0 188.5 jit_solution(12676799592542672888)
XLA Ops:
  6.5 0.0 copy-start
  6.5 0.0 all-reduce.2.cloned.1.call-start
  6.5 1.1 copy.6
  7.6 0.5 collective-permute-start
  8.1 2.9 %collective-permute-start.1 = (f32[48,384]{0,1:T(8,128)S(1)}, f32[48,384]{0,1:T(8,128)S(1)}, u32[]{:S(2)}, u32[]{:S(2)}) collective-permute-start(f32[48,384]{0,1:T(8,128)S(1)} %bitcast.30), channel_id=1, source_target_pairs={{0,28},{4,0},{8,4},{12,8},{16,12},{20,16},{24,20},{28,24},{1,29},{... | collective-permute-start | bytes 221192 | tf_op jit(solution)/shard_map/ppermute | solution.py:21
  11.1 3.3 %collective-permute-done = f32[48,384]{0,1:T(8,128)S(1)} collective-permute-done((f32[48,384]{0,1:T(8,128)S(1)}, f32[48,384]{0,1:T(8,128)S(1)}, u32[]{:S(2)}, u32[]{:S(2)}) %collective-permute-start) | collective-permute-done | bytes 73760 | tf_op jit(solution)/shard_map/ppermute | solution.py:16
  14.4 0.1 collective-permute-start.2
  14.4 0.9 collective-permute-done.1
  15.3 2.8 %collective-permute-start.3 = (f32[48,384]{0,1:T(8,128)S(1)}, f32[48,384]{0,1:T(8,128)S(1)}, u32[]{:S(2)}, u32[]{:S(2)}) collective-permute-start(f32[48,384]{0,1:T(8,128)S(1)} %collective-permute-done.1), channel_id=1, source_target_pairs={{0,28},{4,0},{8,4},{12,8},{16,12},{20,16},{24,20},{28,24},{1,29},{... | collective-permute-start | bytes 221192 | tf_op jit(solution)/shard_map/ppermute | solution.py:21
  18.1 2.2 %collective-permute-done.2 = f32[48,384]{0,1:T(8,128)S(1)} collective-permute-done((f32[48,384]{0,1:T(8,128)S(1)}, f32[48,384]{0,1:T(8,128)S(1)}, u32[]{:S(2)}, u32[]{:S(2)}) %collective-permute-start.2) | collective-permute-done | bytes 73760 | tf_op jit(solution)/shard_map/ppermute | solution.py:16
  20.4 0.0 collective-permute-start.4
  20.4 0.0 copy-done
  20.4 1.9 %fusion = f32[384,384]{1,0:T(8,128)S(1)} fusion(f32[1,1,512,384]{3,2,1,0:T(8,128)S(1)} %copy-done, f32[1,1,512,384]{3,2,1,0:T(8,128)} %param.5), kind=kOutput, calls=%fused_computation.2 | convolution fusion | flops 452984832 | bytes 2162688 | tf_op jit(solution)/shard_map/dot_general | solution.py:29
  22.5 1.5 dynamic_update_slice.24
  24.1 0.0 collective-permute-done.3
  24.1 2.4 %collective-permute-start.5 = (f32[48,384]{0,1:T(8,128)S(1)}, f32[48,384]{0,1:T(8,128)}, u32[]{:S(2)}, u32[]{:S(2)}) collective-permute-start(f32[48,384]{0,1:T(8,128)S(1)} %collective-permute-done.3), channel_id=1, source_target_pairs={{0,28},{4,0},{8,4},{12,8},{16,12},{20,16},{24,20},{28,24},{1,29},{... | collective-permute-start | bytes 221192 | tf_op jit(solution)/shard_map/ppermute | solution.py:21
  26.5 0.0 collective-permute-done.4
  26.5 0.0 collective-permute-start.6
  26.5 1.2 dynamic_update_slice.25
  27.7 1.8 dynamic_update_slice.26
  29.5 1.2 dynamic_update_slice.27
  30.7 1.8 dynamic_update_slice.28
  32.5 0.0 copy-start.2
  32.5 1.8 dynamic_update_slice.29
  34.4 0.0 collective-permute-done.5
  34.4 2.3 %dynamic_update_slice.30 = f32[384,384]{0,1:T(8,128)S(1)} dynamic-update-slice(f32[384,384]{0,1:T(8,128)S(1)} %dynamic_update_slice.29, f32[48,384]{0,1:T(8,128)} %collective-permute-done.5, s32[]{:T(128)S(6)} %select_n.75, s32[]{:T(128)} %constant.60.clone.1) | dynamic-update-slice | bytes 147460 | tf_op jit(solution)/shard_map/dynamic_update_slice | solution.py:22
  36.7 0.0 collective-permute-done.6
  36.7 1.8 dynamic_update_slice.31
  38.6 0.0 copy-done.2
  38.6 0.7 fusion.7
  39.3 1.9 %fusion.16 = f32[384,384]{1,0:T(8,128)} fusion(f32[384,384]{1,0:T(8,128)S(1)} %fusion, f32[384,384]{1,0:T(8,128)S(1)} %fusion.7), kind=kOutput, calls=%fused_computation.22 | convolution fusion | flops 339738624 | bytes 1769472 | tf_op jit(solution)/shard_map/dot_general | solution.py:29
  41.3 0.0 copy-start.3
  41.3 0.0 all-reduce.2.cloned.1.call-update
  41.3 1.0 copy-done.3
  42.3 0.7 fusion.5
  43.0 0.8 fusion.2
  43.9 131.0 %all-reduce.2.cloned.1.call-done = f32[384,384]{1,0:T(8,128)} async-done(((f32[384,384]{1,0:T(8,128)}), f32[384,384]{1,0:T(8,128)}) %all-reduce.2.cloned.1.call-update) | async-done | bytes 589840 | tf_op jit(solution)/shard_map/psum | solution.py:50
  174.9 1.1 neg.3
  176.0 0.0 copy-start.1
  176.0 1.1 copy.7
  177.1 0.1 copy-done.1
  177.1 2.7 %convolution_add_fusion = f32[512,384]{1,0:T(8,128)S(1)} fusion(f32[384,512]{1,0:T(8,128)S(1)} %fusion.2, f32[1,1,512,384]{3,2,1,0:T(8,128)S(1)} %copy-done.1, f32[384,384]{0,1:T(8,128)} %copy.7, s32[384]{0:T(512)S(1)} %iota_add_fusion, f32[384,384]{1,0:T(8,128)} %all-reduce.2.cloned.1.call-done), kind=kOutput, calls=%fused_computation.1 | convolution fusion | flops 454066176 | bytes 3540480 | tf_op jit(solution)/shard_map/dot_general | solution.py:29
  179.9 1.8 convolution_bitcast_fusion
  (2 shorter events, 0.0 us)
Async XLA Ops:
  6.5 13.9 %copy-start = (f32[1,1,512,384]{3,2,1,0:T(8,128)S(1)}, f32[1,1,512,384]{3,2,1,0:T(8,128)}, u32[]{:S(2)}) copy-start(f32[1,1,512,384]{3,2,1,0:T(8,128)} %param.6) | copy-start | bytes 2359300
  6.5 168.4 %all-reduce.2.cloned.1.call-start = ((), (), s32[]{:S(2)}) async-start(), calls=%async_computation | async-start | bytes 1179648 | tf_op jit(solution)/shard_map/psum | solution.py:50
  7.6 6.7 %collective-permute-start = (f32[48,384]{0,1:T(8,128)S(1)}, f32[48,384]{0,1:T(8,128)S(1)}, u32[]{:S(2)}, u32[]{:S(2)}) collective-permute-start(f32[48,384]{0,1:T(8,128)S(1)} %bitcast.29), channel_id=1, source_target_pairs={{0,4},{4,8},{8,12},{12,16},{16,20},{20,24},{24,28},{28,0},{1,5},{5... | collective-permute-start | bytes 221192 | tf_op jit(solution)/shard_map/ppermute | solution.py:16
  8.1 7.2 %collective-permute-start.1 = (f32[48,384]{0,1:T(8,128)S(1)}, f32[48,384]{0,1:T(8,128)S(1)}, u32[]{:S(2)}, u32[]{:S(2)}) collective-permute-start(f32[48,384]{0,1:T(8,128)S(1)} %bitcast.30), channel_id=1, source_target_pairs={{0,28},{4,0},{8,4},{12,8},{16,12},{20,16},{24,20},{28,24},{1,29},{... | collective-permute-start | bytes 221192 | tf_op jit(solution)/shard_map/ppermute | solution.py:21
  14.4 6.0 %collective-permute-start.2 = (f32[48,384]{0,1:T(8,128)S(1)}, f32[48,384]{0,1:T(8,128)S(1)}, u32[]{:S(2)}, u32[]{:S(2)}) collective-permute-start(f32[48,384]{0,1:T(8,128)S(1)} %collective-permute-done), channel_id=1, source_target_pairs={{0,4},{4,8},{8,12},{12,16},{16,20},{20,24},{24,28},{28,0},{1,5},{5... | collective-permute-start | bytes 221192 | tf_op jit(solution)/shard_map/ppermute | solution.py:16
  15.3 8.8 %collective-permute-start.3 = (f32[48,384]{0,1:T(8,128)S(1)}, f32[48,384]{0,1:T(8,128)S(1)}, u32[]{:S(2)}, u32[]{:S(2)}) collective-permute-start(f32[48,384]{0,1:T(8,128)S(1)} %collective-permute-done.1), channel_id=1, source_target_pairs={{0,28},{4,0},{8,4},{12,8},{16,12},{20,16},{24,20},{28,24},{1,29},{... | collective-permute-start | bytes 221192 | tf_op jit(solution)/shard_map/ppermute | solution.py:21
  20.4 6.1 %collective-permute-start.4 = (f32[48,384]{0,1:T(8,128)S(1)}, f32[48,384]{0,1:T(8,128)S(1)}, u32[]{:S(2)}, u32[]{:S(2)}) collective-permute-start(f32[48,384]{0,1:T(8,128)S(1)} %collective-permute-done.2), channel_id=1, source_target_pairs={{0,4},{4,8},{8,12},{12,16},{16,20},{20,24},{24,28},{28,0},{1,5},{5... | collective-permute-start | bytes 221192 | tf_op jit(solution)/shard_map/ppermute | solution.py:16
  24.1 10.3 %collective-permute-start.5 = (f32[48,384]{0,1:T(8,128)S(1)}, f32[48,384]{0,1:T(8,128)}, u32[]{:S(2)}, u32[]{:S(2)}) collective-permute-start(f32[48,384]{0,1:T(8,128)S(1)} %collective-permute-done.3), channel_id=1, source_target_pairs={{0,28},{4,0},{8,4},{12,8},{16,12},{20,16},{24,20},{28,24},{1,29},{... | collective-permute-start | bytes 221192 | tf_op jit(solution)/shard_map/ppermute | solution.py:21
  26.5 10.3 %collective-permute-start.6 = (f32[48,384]{0,1:T(8,128)S(1)}, f32[48,384]{0,1:T(8,128)S(1)}, u32[]{:S(2)}, u32[]{:S(2)}) collective-permute-start(f32[48,384]{0,1:T(8,128)S(1)} %collective-permute-done.4), channel_id=1, source_target_pairs={{0,4},{4,8},{8,12},{12,16},{16,20},{20,24},{24,28},{28,0},{1,5},{5... | collective-permute-start | bytes 221192 | tf_op jit(solution)/shard_map/ppermute | solution.py:16
  32.5 6.1 %copy-start.2 = (f32[1,1,384,384]{3,2,1,0:T(8,128)S(1)}, f32[1,1,384,384]{3,2,1,0:T(8,128)}, u32[]{:S(2)}) copy-start(f32[1,1,384,384]{3,2,1,0:T(8,128)} %param.8) | copy-start | bytes 1769476
  41.3 1.1 copy-start.3
  176.0 1.1 copy-start.1
Sparse Core Ops, SparseCore 0:
  41.4 133.4 all-reduce.1
